TPU v7x, 256 devices: a whole 4x4x8 slice. The times are simulated.
256 devices in a mesh: seq: 32 (over y, z), head: 8 (over x, core).
Axes of the slice: x: 4, y: 4, z: 8, core: 2. Of those that a mesh axis runs over, the one named last changes fastest.
Arguments:
- tokens: bfloat16 [16384, 2048], P('seq'), may hold values from -24 to 24
- w_query: bfloat16 [2048, 2048], P(None, 'head'), may hold values from -0.125 to 0.125
- w_key: bfloat16 [2048, 2048], P(None, 'head'), may hold values from -0.125 to 0.125
- w_value: bfloat16 [2048, 2048], P(None, 'head'), may hold values from -0.125 to 0.125
- w_out: bfloat16 [2048, 2048], P('head'), may hold values from -0.125 to 0.125
- shared_gate: bfloat16 [2048, 1024], P(None, 'head'), may hold values from -0.125 to 0.125
- shared_up: bfloat16 [2048, 1024], P(None, 'head'), may hold values from -0.125 to 0.125
- shared_down: bfloat16 [1024, 2048], P('head'), may hold values from -0.1875 to 0.1875
- expert_gate: bfloat16 [64, 2048, 1024], P('seq', None, 'head'), may hold values from -0.125 to 0.125
- expert_up: bfloat16 [64, 2048, 1024], P('seq', None, 'head'), may hold values from -0.125 to 0.125
- expert_down: bfloat16 [64, 1024, 2048], P('seq', 'head'), may hold values from -0.1875 to 0.1875
- expert_ids: int32 [16384, 1], P('seq'), may hold values from 0 to 63; in each aligned block of 512 rows (0 to 511, 512 to 1023, ...) at most 16 rows name the same one
Outputs:
- output: bfloat16 [16384, 2048], P('seq', 'head')
Inputs may be any that keep to these rules, and one draw needn't show every extreme that they name: `expert_ids`: among the 512 tokens of one index of seq (aligned blocks of the sequence) at most 16 name the same expert, and in some block of every draw one expert is named by exactly 16 tokens.
All inputs are finite; a program needn't handle non-finite values.
Results may differ from a plain program's by a relative error of at most 0.015.
Values may be sent and summed in bfloat16 or wider, within the bound.
A program may use at most 128 MiB of HBM per device.

v0:
```python
import jax
import jax.numpy as jnp
from jax import lax
from jax.sharding import PartitionSpec as P

HD = 128
EXPERTS = 64
CAP = 16
F32 = jnp.float32
BF16 = jnp.bfloat16


def dot(a, b):
    return jnp.dot(a, b, preferred_element_type=F32)


def two_part(values):
    high = values.astype(BF16)
    return (high, (values - high.astype(F32)).astype(BF16))


def head_columns(weights):
    return lax.all_to_all(weights, "head", split_axis=1, concat_axis=0, tiled=True)


def gather_columns(block):
    return lax.all_gather(block, "head", axis=1, tiled=True)


def carried_state(local_state):
    shape = local_state.shape
    length = lax.axis_size("seq")
    chunks = local_state.reshape(length, -1, HD)
    mine = lax.all_to_all(chunks, "seq", split_axis=0, concat_axis=0, tiled=True)
    earlier = jnp.arange(length)[:, None] > jnp.arange(length)[None, :]
    before = jnp.sum(jnp.where(earlier[:, :, None, None], mine[None], 0.0), axis=1)
    back = lax.all_to_all(before, "seq", split_axis=0, concat_axis=0, tiled=True)
    return back.reshape(shape)


def row_scale(rows):
    wide = rows.astype(F32)
    return lax.rsqrt(jnp.mean(wide * wide, axis=-1, keepdims=True) + 1e-06)


def shards(
    tokens,
    w_query,
    w_key,
    w_value,
    w_out,
    shared_gate,
    shared_up,
    shared_down,
    expert_gate,
    expert_up,
    expert_down,
    expert_ids,
):
    rows, width = tokens.shape
    heads = w_query.shape[1] // HD
    owned = expert_gate.shape[0]
    sources = lax.axis_size("seq")
    experts = owned * sources
    cols = width // lax.axis_size("head")
    head = lax.axis_index("head")
    out_cols = head_columns(w_out)
    shared_cols = head_columns(shared_down)
    expert_cols = lax.all_to_all(expert_down, "head", split_axis=2, concat_axis=1, tiled=True)
    inputs = tokens.astype(F32)
    normed = (inputs * row_scale(tokens)).astype(BF16)
    query = dot(normed, w_query).astype(BF16).reshape(rows, heads, HD)
    key = dot(normed, w_key).astype(BF16).reshape(rows, heads, HD)
    value = dot(normed, w_value).astype(BF16).reshape(rows, heads, HD)
    state = jnp.einsum("thd,the->hde", key, value, preferred_element_type=F32)
    carried = carried_state(state)
    causal = jnp.arange(rows)[:, None] >= jnp.arange(rows)[None, :]
    scores = jnp.einsum("thd,shd->hts", query, key, preferred_element_type=F32)
    scores = two_part(jnp.where(causal[None], scores, 0.0))
    carried = two_part(carried)
    attended = sum(
        (jnp.einsum("hts,shd->thd", part, value, preferred_element_type=F32) for part in scores)
    ) + sum(
        (jnp.einsum("thd,hde->the", query, part, preferred_element_type=F32) for part in carried)
    )
    head_normed = (
        (attended * lax.rsqrt(jnp.mean(attended * attended, axis=-1, keepdims=True) + 1e-06))
        .astype(BF16)
        .reshape(rows, heads * HD)
    )
    own_tokens = lax.dynamic_slice_in_dim(tokens, head * cols, cols, 1)
    residual = own_tokens.astype(F32) + dot(gather_columns(head_normed), out_cols)
    sent = residual.astype(BF16)
    expert_of = expert_ids[:, 0]
    same = (expert_of[:, None] == expert_of[None, :]) & causal
    rank = jnp.sum(same.astype(jnp.int32), axis=1) - 1
    slot = expert_of * CAP + rank
    chosen = jnp.arange(experts * CAP, dtype=jnp.int32)[:, None] == slot[None, :]
    chosen = chosen.astype(BF16)
    outgoing = dot(chosen, sent).astype(BF16).reshape(sources, owned, CAP, cols)
    arrived = lax.all_to_all(outgoing, "seq", split_axis=0, concat_axis=0, tiled=True)
    arrived = arrived.transpose(1, 0, 2, 3).reshape(owned * sources * CAP, cols)
    routed_in = gather_columns(arrived)
    middle = gather_columns(sent)
    scale = row_scale(middle)
    shared_hidden = (
        jax.nn.silu(dot(middle, shared_gate) * scale) * (dot(middle, shared_up) * scale)
    ).astype(BF16)
    scale = row_scale(routed_in).reshape(owned, sources * CAP, 1)
    routed_in = routed_in.reshape(owned, sources * CAP, width)
    gate = jnp.einsum("erd,edf->erf", routed_in, expert_gate, preferred_element_type=F32)
    up = jnp.einsum("erd,edf->erf", routed_in, expert_up, preferred_element_type=F32)
    routed_hidden = (jax.nn.silu(gate * scale) * (up * scale)).astype(BF16)
    both = jnp.concatenate([shared_hidden, routed_hidden.reshape(owned * sources * CAP, -1)])
    both = gather_columns(both)
    shared_out = dot(both[:rows], shared_cols)
    routed_out = jnp.einsum(
        "erf,efd->erd",
        both[rows:].reshape(owned, sources * CAP, -1),
        expert_cols,
        preferred_element_type=F32,
    ).astype(BF16)
    routed_out = routed_out.reshape(owned, sources, CAP, cols).transpose(1, 0, 2, 3)
    returned = lax.all_to_all(routed_out, "seq", split_axis=0, concat_axis=0, tiled=True)
    returned = returned.reshape(experts * CAP, cols)
    routed = lax.dot_general(chosen, returned, (((0,), (0,)), ((), ())), preferred_element_type=F32)
    return (residual + shared_out + routed).astype(BF16)


def solution(mesh):
    return jax.shard_map(
        shards,
        mesh=mesh,
        in_specs=(
            P("seq", None),
            P(None, "head"),
            P(None, "head"),
            P(None, "head"),
            P("head", None),
            P(None, "head"),
            P(None, "head"),
            P("head", None),
            P("seq", None, "head"),
            P("seq", None, "head"),
            P("seq", "head", None),
            P("seq", None),
        ),
        out_specs=P("seq", "head"),
        check_vma=False,
    )
```

profile of v0, /device:TPU:32, one launch (start us, length us, event | category | flops | bytes accessed | tf_op | source)
XLA Modules:
  0.0 251.0 jit_solution(1890059835473310391)
XLA Ops:
  6.5 2.2 fusion
  8.8 0.3 copy-done.5
  9.1 0.9 convolution_convert_fusion.1
  10.0 0.3 copy-done.17
  10.3 0.9 convolution_convert_fusion.3
  11.3 0.9 fusion.31
  12.1 11.4 %all-to-all-start = ((f32[32,8,128]{2,1,0:T(8,128)}), f32[32,8,128]{2,1,0:T(8,128)S(1)}, u32[]{:S(2)}, u32[]{:S(2)}) async-start(f32[32,8,128]{2,1,0:T(8,128)} %bitcast.3), calls=%async_computation | async-start | bytes 262144 | tf_op jit(solution)/shard_map/all_to_all | solution.py:34
  23.5 0.8 iota_compare_fusion.5
  24.3 2.1 convolution_convert_fusion.2
  26.5 0.7 copy-done.4
  27.2 0.5 fusion.30
  27.6 5.7 %all-to-all-done = f32[32,8,128]{2,1,0:T(8,128)S(1)} async-done(((f32[32,8,128]{2,1,0:T(8,128)}), f32[32,8,128]{2,1,0:T(8,128)S(1)}, u32[]{:S(2)}, u32[]{:S(2)}) %all-to-all-start) | async-done | bytes 131104 | tf_op jit(solution)/shard_map/all_to_all | solution.py:34
  33.3 2.1 select_reduce_fusion
  35.4 4.3 %all-to-all-start.1 = ((f32[32,8,128]{2,1,0:T(8,128)}), f32[32,8,128]{2,1,0:T(8,128)S(1)}, u32[]{:S(2)}, u32[]{:S(2)}) async-start(f32[32,8,128]{2,1,0:T(8,128)} %select_reduce_fusion), calls=%async_computation.1 | async-start | bytes 262144 | tf_op jit(solution)/shard_map/all_to_all | solution.py:37
  39.6 0.0 all-gather.5.cloned.1.call-start
  39.7 2.3 fusion.4
  42.0 7.5 %all-to-all-done.1 = f32[32,8,128]{2,1,0:T(8,128)S(1)} async-done(((f32[32,8,128]{2,1,0:T(8,128)}), f32[32,8,128]{2,1,0:T(8,128)S(1)}, u32[]{:S(2)}, u32[]{:S(2)}) %all-to-all-start.1) | async-done | bytes 131104 | tf_op jit(solution)/shard_map/all_to_all | solution.py:37
  49.5 0.7 copy-done.14
  50.1 1.0 copy.61
  51.1 1.2 fusion.22
  52.4 1.2 convolution_add_fusion.3
  53.5 0.6 multiply_reduce_fusion.2
  54.2 0.7 multiply_convert_fusion
  54.9 0.0 all-gather.5.cloned.1.call-update
  54.9 2.3 copy.65
  57.2 4.3 %all-to-all-start.2 = ((bf16[256,8,256]{0,2,1:T(8,128)(2,1)}), bf16[256,8,256]{0,2,1:T(8,128)(2,1)S(1)}, u32[]{:S(2)}, u32[]{:S(2)}) async-start(bf16[256,8,256]{0,2,1:T(8,128)(2,1)} %bitcast.7), calls=%async_computation.2 | async-start | bytes 2097152 | tf_op jit(solution)/shard_map/all_to_all | solution.py:23
  61.5 0.0 all-gather.7.cloned.1.call-start
  61.6 24.3 %all-to-all-done.2 = bf16[256,8,256]{0,2,1:T(8,128)(2,1)S(1)} async-done(((bf16[256,8,256]{0,2,1:T(8,128)(2,1)}), bf16[256,8,256]{0,2,1:T(8,128)(2,1)S(1)}, u32[]{:S(2)}, u32[]{:S(2)}) %all-to-all-start.2) | async-done | bytes 1048608 | tf_op jit(solution)/shard_map/all_to_all | solution.py:23
  85.9 0.5 copy.66
  86.4 0.0 all-gather.5.cloned.1.call-done
  86.4 3.2 %fusion.29 = (bf16[512,256]{1,0:T(8,128)(2,1)}, f32[512,256]{1,0:T(8,128)}) fusion(bf16[512,2048]{0,1:T(8,128)(2,1)} %all-gather.5.cloned.1.call-done, bf16[2048,256]{1,0:T(8,128)(2,1)S(1)} %bitcast.73, bf16[512,2048]{1,0:T(8,128)(2,1)} %param.12, s32[]{:T(128)S(6)} %select_n.11), kind=kOutput, calls=%fused_computation.59 | convolution fusion | flops 537264128 | bytes 4194308 | tf_op jit(solution)/shard_map/dot_general | solution.py:14
  89.7 0.0 all-gather.7.cloned.1.call-update
  89.7 0.0 all-gather.9.cloned.1.call-start
  89.7 0.2 convert_reduce_fusion
  90.0 1.4 fusion.5
  91.4 23.0 %all_to_all.76 = bf16[32,2,16,256]{3,2,1,0:T(8,128)(2,1)S(1)} all-to-all(bf16[32,2,16,256]{3,2,1,0:T(8,128)(2,1)S(1)} %bitcast.77), channel_id=1, replica_groups=mesh['seq'=32,'head'=8] {'seq'}, dimensions={0} | all-to-all | bytes 1048576 | tf_op jit(solution)/shard_map/all_to_all | solution.py:101
  114.5 0.8 copy.67
  115.3 0.2 all-gather.11.cloned.1.call-start
  115.5 0.0 all-gather.7.cloned.1.call-done
  115.6 2.2 multiply_reduce_fusion.1
  117.8 0.7 convolution_multiply_fusion.3
  118.6 0.7 fusion.13
  119.3 36.5 %all-gather.9.cloned.1.call-done = bf16[1024,2048]{1,0:T(8,128)(2,1)} async-done(((bf16[1024,256]{1,0:T(8,128)(2,1)}), bf16[1024,2048]{1,0:T(8,128)(2,1)}) %all-gather.9.cloned.1.call-update) | async-done | bytes 4194320 | tf_op jit(solution)/shard_map/all_gather | solution.py:27
  155.7 3.1 %multiply_reduce_fusion = f32[1024]{0:T(1024)S(1)} fusion(bf16[1024,2048]{1,0:T(8,128)(2,1)} %all-gather.9.cloned.1.call-done), kind=kLoop, calls=%fused_computation | loop fusion | flops 6290432 | bytes 4198400 | tf_op jit(solution)/shard_map/reduce_sum | solution.py:43
  158.9 3.6 %convolution_multiply_fusion.1 = f32[2,512,128]{2,1,0:T(8,128)S(1)} fusion(bf16[2,512,2048]{2,1,0:T(8,128)(2,1)} %bitcast.57, bf16[2,2048,128]{2,1,0:T(8,128)(2,1)S(1)} %copy-done.11, f32[2,512]{1,0:T(2,128)S(1)} %rsqrt.40), kind=kOutput, calls=%fused_computation.23 | convolution fusion | flops 537001984 | bytes 5771264 | tf_op jit(solution)/shard_map/erd,edf->erf/dot_general | solution.py:111
  162.5 0.1 copy-done.18
  162.6 1.3 fusion.10
  163.9 0.8 pad_maximum_fusion
  164.7 2.0 copy.70
  166.7 3.9 %all-to-all-start.5 = ((bf16[2,128,2048]{1,0,2:T(2,128)(2,1)}), bf16[2,128,2048]{1,0,2:T(2,128)(2,1)S(1)}, u32[]{:S(2)}, u32[]{:S(2)}) async-start(bf16[2,128,2048]{1,0,2:T(2,128)(2,1)} %copy.70), calls=%async_computation.5 | async-start | bytes 2097152 | tf_op jit(solution)/shard_map/all_to_all | solution.py:69
  170.7 1.0 copy.68
  171.7 19.1 %all-to-all-done.5 = bf16[2,128,2048]{1,0,2:T(2,128)(2,1)S(1)} async-done(((bf16[2,128,2048]{1,0,2:T(2,128)(2,1)}), bf16[2,128,2048]{1,0,2:T(2,128)(2,1)S(1)}, u32[]{:S(2)}, u32[]{:S(2)}) %all-to-all-start.5) | async-done | bytes 1048608 | tf_op jit(solution)/shard_map/all_to_all | solution.py:69
  190.8 4.1 %all-to-all-start.4 = ((bf16[128,8,256]{0,2,1:T(8,128)(2,1)}), bf16[128,8,256]{0,2,1:T(8,128)(2,1)}, u32[]{:S(2)}, u32[]{:S(2)}) async-start(bf16[128,8,256]{0,2,1:T(8,128)(2,1)} %bitcast.16), calls=%async_computation.4 | async-start | bytes 1048576 | tf_op jit(solution)/shard_map/all_to_all | solution.py:23
  195.0 2.0 copy.71
  197.0 12.7 %all-gather.11.cloned.1.call-done = bf16[1536,1024]{1,0:T(8,128)(2,1)} async-done(((bf16[1536,128]{1,0:T(8,128)(2,1)}), bf16[1536,1024]{1,0:T(8,128)(2,1)}) %all-gather.11.cloned.1.call-update) | async-done | bytes 3145744 | tf_op jit(solution)/shard_map/all_gather | solution.py:27
  209.7 1.6 slice-done
  211.2 0.3 copy-done.10
  211.5 0.7 convolution_convert_fusion
  212.2 0.9 copy.79
  213.1 10.2 %all-to-all-start.6 = ((bf16[32,2,16,256]{3,2,1,0:T(8,128)(2,1)}), bf16[32,2,16,256]{3,2,1,0:T(8,128)(2,1)S(1)}, u32[]{:S(2)}, u32[]{:S(2)}) async-start(bf16[32,2,16,256]{3,2,1,0:T(8,128)(2,1)} %bitcast.56), calls=%async_computation.6 | async-start | bytes 1048576 | tf_op jit(solution)/shard_map/all_to_all | solution.py:124
  223.3 1.2 copy.69
  224.6 16.8 %all-to-all-done.6 = bf16[32,2,16,256]{3,2,1,0:T(8,128)(2,1)S(1)} async-done(((bf16[32,2,16,256]{3,2,1,0:T(8,128)(2,1)}), bf16[32,2,16,256]{3,2,1,0:T(8,128)(2,1)S(1)}, u32[]{:S(2)}, u32[]{:S(2)}) %all-to-all-start.6) | async-done | bytes 524320 | tf_op jit(solution)/shard_map/all_to_all | solution.py:124
  241.4 0.7 fusion.2
  242.1 2.4 fusion.11
  (45 shorter events, 0.2 us)
Async XLA Ops:
  6.5 2.2 copy-start
  6.5 2.5 %copy-start.5 = (bf16[512,2048]{1,0:T(8,128)(2,1)S(1)}, bf16[512,2048]{1,0:T(8,128)(2,1)}, u32[]{:S(2)}) copy-start(bf16[512,2048]{1,0:T(8,128)(2,1)} %param.12) | copy-start | bytes 6291460
  9.1 1.2 copy-start.17
  10.3 0.9 copy-start.7
  12.1 21.2 %all-to-all-start = ((f32[32,8,128]{2,1,0:T(8,128)}), f32[32,8,128]{2,1,0:T(8,128)S(1)}, u32[]{:S(2)}, u32[]{:S(2)}) async-start(f32[32,8,128]{2,1,0:T(8,128)} %bitcast.3), calls=%async_computation | async-start | bytes 262144 | tf_op jit(solution)/shard_map/all_to_all | solution.py:34
  24.3 2.8 %copy-start.8 = (bf16[512,256]{0,1:T(8,128)(2,1)S(1)}, bf16[512,256]{0,1:T(8,128)(2,1)}, u32[]{:S(2)}) copy-start(bf16[512,256]{0,1:T(8,128)(2,1)} %copy-done.7) | copy-start | bytes 786436
  26.4 0.7 copy-start.4
  35.4 14.1 %all-to-all-start.1 = ((f32[32,8,128]{2,1,0:T(8,128)}), f32[32,8,128]{2,1,0:T(8,128)S(1)}, u32[]{:S(2)}, u32[]{:S(2)}) async-start(f32[32,8,128]{2,1,0:T(8,128)} %select_reduce_fusion), calls=%async_computation.1 | async-start | bytes 262144 | tf_op jit(solution)/shard_map/all_to_all | solution.py:37
  39.6 46.8 %all-gather.5.cloned.1.call-start = ((), (), s32[]{:S(2)}) async-start(), calls=%async_computation.7 | async-start | bytes 2359296 | tf_op jit(solution)/shard_map/all_gather | solution.py:27
  49.4 0.7 copy-start.14
  51.1 2.4 copy-start.3
  51.1 2.4 copy-start.6
  57.2 28.7 %all-to-all-start.2 = ((bf16[256,8,256]{0,2,1:T(8,128)(2,1)}), bf16[256,8,256]{0,2,1:T(8,128)(2,1)S(1)}, u32[]{:S(2)}, u32[]{:S(2)}) async-start(bf16[256,8,256]{0,2,1:T(8,128)(2,1)} %bitcast.7), calls=%async_computation.2 | async-start | bytes 2097152 | tf_op jit(solution)/shard_map/all_to_all | solution.py:23
  61.5 54.1 %all-gather.7.cloned.1.call-start = ((), (), s32[]{:S(2)}) async-start(), calls=%async_computation.8 | async-start | bytes 2359296 | tf_op jit(solution)/shard_map/all_gather | solution.py:27
  86.4 3.3 %copy-start.16 = (s32[512,1]{0,1:T(1,128)S(1)}, s32[512,1]{0,1:T(1,128)}, u32[]{:S(2)}) copy-start(s32[512,1]{0,1:T(1,128)} %param.23) | copy-start | bytes 6148
  89.7 66.1 %all-gather.9.cloned.1.call-start = ((), (), s32[]{:S(2)}) async-start(), calls=%async_computation.9 | async-start | bytes 4718592 | tf_op jit(solution)/shard_map/all_gather | solution.py:27
  114.5 3.4 %copy-start.12 = (bf16[2048,128]{1,0:T(8,128)(2,1)S(1)}, bf16[2048,128]{1,0:T(8,128)(2,1)}, u32[]{:S(2)}) copy-start(bf16[2048,128]{1,0:T(8,128)(2,1)} %param.17) | copy-start | bytes 1572868
  115.3 3.3 %copy-start.19 = (bf16[2048,128]{1,0:T(8,128)(2,1)S(1)}, bf16[2048,128]{1,0:T(8,128)(2,1)}, u32[]{:S(2)}) copy-start(bf16[2048,128]{1,0:T(8,128)(2,1)} %param.18) | copy-start | bytes 1572868
  115.3 94.3 %all-gather.11.cloned.1.call-start = ((), (), s32[]{:S(2)}) async-start(), calls=%async_computation.10 | async-start | bytes 3538944 | tf_op jit(solution)/shard_map/all_gather | solution.py:27
  115.6 2.3 copy-start.2
  119.3 39.6 %copy-start.11 = (bf16[2,2048,128]{2,1,0:T(8,128)(2,1)S(1)}, bf16[2,2048,128]{2,1,0:T(8,128)(2,1)}, u32[]{:S(2)}) copy-start(bf16[2,2048,128]{2,1,0:T(8,128)(2,1)} %param.20) | copy-start | bytes 3145732
  158.9 3.6 %copy-start.1 = (bf16[1024,2048]{1,0:T(8,128)(2,1)S(1)}, bf16[1024,2048]{1,0:T(8,128)(2,1)}, u32[]{:S(2)}) copy-start(bf16[1024,2048]{1,0:T(8,128)(2,1)} %all-gather.9.cloned.1.call-done) | copy-start | bytes 12582916
  158.9 3.7 %copy-start.18 = (bf16[2,2048,128]{2,1,0:T(8,128)(2,1)S(1)}, bf16[2,2048,128]{2,1,0:T(8,128)(2,1)}, u32[]{:S(2)}) copy-start(bf16[2,2048,128]{2,1,0:T(8,128)(2,1)} %param.21) | copy-start | bytes 3145732
  162.6 2.1 copy-start.9
  164.7 6.0 %copy-start.13 = (bf16[128,2048]{1,0:T(8,128)(2,1)S(1)}, bf16[128,2048]{1,0:T(8,128)(2,1)}, u32[]{:S(2)}) copy-start(bf16[128,2048]{1,0:T(8,128)(2,1)} %param.19) | copy-start | bytes 1572868
  166.7 24.1 %all-to-all-start.5 = ((bf16[2,128,2048]{1,0,2:T(2,128)(2,1)}), bf16[2,128,2048]{1,0,2:T(2,128)(2,1)S(1)}, u32[]{:S(2)}, u32[]{:S(2)}) async-start(bf16[2,128,2048]{1,0,2:T(2,128)(2,1)} %copy.70), calls=%async_computation.5 | async-start | bytes 2097152 | tf_op jit(solution)/shard_map/all_to_all | solution.py:69
  190.8 22.3 %all-to-all-start.4 = ((bf16[128,8,256]{0,2,1:T(8,128)(2,1)}), bf16[128,8,256]{0,2,1:T(8,128)(2,1)}, u32[]{:S(2)}, u32[]{:S(2)}) async-start(bf16[128,8,256]{0,2,1:T(8,128)(2,1)} %bitcast.16), calls=%async_computation.4 | async-start | bytes 1048576 | tf_op jit(solution)/shard_map/all_to_all | solution.py:23
  209.7 1.6 slice-start
  209.7 1.9 copy-start.10
  213.1 29.0 %copy-start.15 = (f32[512,256]{1,0:T(8,128)S(1)}, f32[512,256]{1,0:T(8,128)}, u32[]{:S(2)}) copy-start(f32[512,256]{1,0:T(8,128)} %get-tuple-element.8) | copy-start | bytes 1572868
  213.1 28.3 %all-to-all-start.6 = ((bf16[32,2,16,256]{3,2,1,0:T(8,128)(2,1)}), bf16[32,2,16,256]{3,2,1,0:T(8,128)(2,1)S(1)}, u32[]{:S(2)}, u32[]{:S(2)}) async-start(bf16[32,2,16,256]{3,2,1,0:T(8,128)(2,1)} %bitcast.56), calls=%async_computation.6 | async-start | bytes 1048576 | tf_op jit(solution)/shard_map/all_to_all | solution.py:124
Sparse Core Ops, SparseCore 0:
  55.1 29.5 all-gather.4
  89.8 25.0 all-gather.6
  116.7 39.0 all-gather.8
  164.8 44.8 all-gather.10
where the time goes:
time: 252 us; the launch traced here: 251 us
  waiting for transfers between devices  123 us (49%)
  starting transfers between devices  38.6 us (15%)
  matrix products  25.3 us (10%)
  blocking collectives  23 us (9%)
  local copies, waits for them, and re-layouts  15.8 us (6%)
  between operations  13.5 us (5%)
  other arithmetic  12.2 us (5%)
    all_gather x4, waiting for transfers between devices, gather_columns(): return lax.all_gather(block, 'head', axis=1, tiled=True)  49.2 us
    all_to_all x2, waiting for transfers between devices, head_columns(): lax.all_to_all(weights, 'head', split_axis=1, concat_axis=0, tiled=True)  24.3 us
    all_to_all x1, blocking collectives, shards(): lax.all_to_all(outgoing, 'seq', split_axis=0, concat_axis=0, tiled=True)  23 us
    all_to_all x1, waiting for transfers between devices, shards(): lax.all_to_all(expert_down, 'head', split_axis=2, concat_axis=1, tiled=True)  19.1 us
    all_to_all x1, waiting for transfers between devices, shards(): lax.all_to_all(routed_out, 'seq', split_axis=0, concat_axis=0, tiled=True)  16.8 us
    dot_general x8, matrix products, dot(): return jnp.dot(a, b, preferred_element_type=F32)  12.4 us
    all_to_all x1, starting transfers between devices, carried_state(): lax.all_to_all(chunks, 'seq', split_axis=0, concat_axis=0, tiled=True)  11.4 us
    all_to_all x1, starting transfers between devices, shards(): lax.all_to_all(routed_out, 'seq', split_axis=0, concat_axis=0, tiled=True)  10.2 us
  transfers between devices with their start and end apart: 10, of which 7 were waited for; matrix products, arithmetic and copies ran while one was open for 9% of the time, Pallas kernels for 0%

commit v1 on v0

--- a/solution.py
+++ b/solution.py
@@ -8,6 +8,12 @@
 CAP = 16
 F32 = jnp.float32
 BF16 = jnp.bfloat16
+
+
+def outputs_enter(w_in):
+    y2 = jnp.stack([w_in for _ in range(jax.lax.axis_size("head"))], axis=0)
+    upper = jax.lax.all_to_all(y2, "head", split_axis=0, concat_axis=0)
+    return jnp.concatenate(upper, 1)
 
 
 def dot(a, b):
@@ -24,7 +30,7 @@
 
 
 def gather_columns(block):
-    return lax.all_gather(block, "head", axis=1, tiled=True)
+    return outputs_enter(block)
 
 
 def carried_state(local_state):

time: 252 us -> 325 us (1.29)
  waiting for transfers between devices: 123 us -> 195 us
  blocking collectives: 23 us -> 0 us
  local copies, waits for them, and re-layouts: 15.8 us -> 38.1 us
  starting transfers between devices: 38.6 us -> 56.5 us
  between operations: 13.5 us -> 0.41 us
    all_to_all x0 -> x5, waiting for transfers between devices: none -> 154 us  [the longest x4 136 us: outputs_enter(): upper = jax.lax.all_to_all(y2, 'head', split_axis=0, concat_axis=0)]
    all_gather x4 -> x0, waiting for transfers between devices: 49.2 us -> none  [gather_columns(): return lax.all_gather(block, 'head', axis=1, tiled=True)]
    all_to_all x1 -> x0, blocking collectives: 23 us -> none  [shards(): lax.all_to_all(outgoing, 'seq', split_axis=0, concat_axis=0, tiled=True)]
    all_to_all x0 -> x5, starting transfers between devices: none -> 21.3 us  [the longest x4 16.9 us: outputs_enter(): upper = jax.lax.all_to_all(y2, 'head', split_axis=0, concat_axis=0)]
    all_to_all x1, waiting for transfers between devices: 19.1 us -> 0.01 us  [shards(): lax.all_to_all(expert_down, 'head', split_axis=2, concat_axis=1, tiled=True)]
    another operation x0 -> x6, local copies, waits for them, and re-layouts: none -> 14.9 us  [the longest x5 7.47 us: outputs_enter(): y2 = jnp.stack([w_in for _ in range(jax.lax.axis_size('head'))], axis=0)]
    all_to_all x2, waiting for transfers between devices: 24.3 us -> 14.1 us  [head_columns(): lax.all_to_all(weights, 'head', split_axis=1, concat_axis=0, tiled=True)]
    reshape x0 -> x2, local copies, waits for them, and re-layouts: none -> 8.86 us  [the longest x1 6.57 us: outputs_enter(): return jnp.concatenate(upper, 1)]
  transfers between devices with their start and end apart: 10 -> 11, of which waited for: 7 -> 9; matrix products, arithmetic and copies ran while one was open for 9% -> 15% of each run, Pallas kernels for 0% -> 0%
where the time goes in v1:
time: 325 us; the launch traced here: 324 us
  waiting for transfers between devices  195 us (60%)
  starting transfers between devices  56.5 us (17%)
  local copies, waits for them, and re-layouts  38.1 us (12%)
  matrix products  24.3 us (7%)
  other arithmetic  9.01 us (3%)
    all_to_all x4, waiting for transfers between devices, outputs_enter(): upper = jax.lax.all_to_all(y2, 'head', split_axis=0, concat_axis=0)  136 us
    all_to_all x1, waiting for transfers between devices, shards(): lax.all_to_all(outgoing, 'seq', split_axis=0, concat_axis=0, tiled=True)  17.6 us
    all_to_all x4, starting transfers between devices, outputs_enter(): upper = jax.lax.all_to_all(y2, 'head', split_axis=0, concat_axis=0)  16.9 us
    all_to_all x1, waiting for transfers between devices, shards(): lax.all_to_all(routed_out, 'seq', split_axis=0, concat_axis=0, tiled=True)  16.2 us
    all_to_all x2, waiting for transfers between devices, head_columns(): lax.all_to_all(weights, 'head', split_axis=1, concat_axis=0, tiled=True)  14.1 us
    all_to_all x1, starting transfers between devices, carried_state(): lax.all_to_all(chunks, 'seq', split_axis=0, concat_axis=0, tiled=True)  11.4 us
    dot_general x8, matrix products, dot(): return jnp.dot(a, b, preferred_element_type=F32)  10.8 us
    all_to_all x2, starting transfers between devices, head_columns(): lax.all_to_all(weights, 'head', split_axis=1, concat_axis=0, tiled=True)  8.45 us
  transfers between devices with their start and end apart: 11, of which 9 were waited for; matrix products, arithmetic and copies ran while one was open for 15% of the time, Pallas kernels for 0%

profile of v1, /device:TPU:32, one launch (start us, length us, event | category | flops | bytes accessed | tf_op | source)
XLA Modules:
  0.0 323.7 jit_solution(11328402177264562705)
XLA Ops:
  0.0 2.2 fusion
  2.2 0.3 copy-done.5
  2.6 0.9 convolution_convert_fusion.1
  3.4 0.3 copy-done.15
  3.8 0.9 convolution_convert_fusion.3
  4.7 0.9 fusion.42
  5.6 11.4 %all-to-all-start = ((f32[32,8,128]{2,1,0:T(8,128)}), f32[32,8,128]{2,1,0:T(8,128)S(1)}, u32[]{:S(2)}, u32[]{:S(2)}) async-start(f32[32,8,128]{2,1,0:T(8,128)} %bitcast.3), calls=%async_computation | async-start | bytes 262144 | tf_op jit(solution)/shard_map/all_to_all | solution.py:40
  17.0 0.8 iota_compare_fusion.9
  17.8 1.6 convolution_convert_fusion.2
  19.3 1.5 copy.64
  20.8 1.3 copy.65
  22.1 1.5 fusion.41
  23.7 3.1 all-to-all-done
  26.8 2.0 select_reduce_fusion
  28.8 6.7 %all-to-all-start.1 = ((f32[32,8,128]{2,1,0:T(8,128)}), f32[32,8,128]{2,1,0:T(8,128)S(1)}, u32[]{:S(2)}, u32[]{:S(2)}) async-start(f32[32,8,128]{2,1,0:T(8,128)} %select_reduce_fusion), calls=%async_computation.1 | async-start | bytes 262144 | tf_op jit(solution)/shard_map/all_to_all | solution.py:43
  35.6 1.3 fusion.6
  36.9 8.4 %all-to-all-done.1 = f32[32,8,128]{2,1,0:T(8,128)S(1)} async-done(((f32[32,8,128]{2,1,0:T(8,128)}), f32[32,8,128]{2,1,0:T(8,128)S(1)}, u32[]{:S(2)}, u32[]{:S(2)}) %all-to-all-start.1) | async-done | bytes 131104 | tf_op jit(solution)/shard_map/all_to_all | solution.py:43
  45.3 4.3 %all-to-all-start.3 = ((bf16[256,8,256]{2,0,1:T(8,128)(2,1)}), bf16[256,8,256]{2,0,1:T(8,128)(2,1)}, u32[]{:S(2)}, u32[]{:S(2)}) async-start(bf16[256,8,256]{2,0,1:T(8,128)(2,1)} %copy.65), calls=%async_computation.3 | async-start | bytes 2097152 | tf_op jit(solution)/shard_map/all_to_all | solution.py:29
  49.7 0.2 fusion.33
  49.9 0.2 convolution_add_fusion.1
  50.1 0.6 copy-done.6
  50.7 0.6 multiply_reduce_fusion.2
  51.6 14.1 %all-to-all-done.3 = bf16[256,8,256]{2,0,1:T(8,128)(2,1)} async-done(((bf16[256,8,256]{2,0,1:T(8,128)(2,1)}), bf16[256,8,256]{2,0,1:T(8,128)(2,1)}, u32[]{:S(2)}, u32[]{:S(2)}) %all-to-all-start.3) | async-done | bytes 1048608 | tf_op jit(solution)/shard_map/all_to_all | solution.py:29
  65.6 1.5 stack.8
  67.1 3.7 %all-to-all-start.2 = ((bf16[8,512,256]{2,1,0:T(8,128)(2,1)}), bf16[8,512,256]{2,1,0:T(8,128)(2,1)S(1)}, u32[]{:S(2)}, u32[]{:S(2)}) async-start(bf16[8,512,256]{2,1,0:T(8,128)(2,1)} %stack.8), calls=%async_computation.2 | async-start | bytes 4194304 | tf_op jit(solution)/shard_map/all_to_all | solution.py:15
  70.9 0.2 convert_reduce_fusion
  71.1 26.8 %all-to-all-done.2 = bf16[8,512,256]{2,1,0:T(8,128)(2,1)S(1)} async-done(((bf16[8,512,256]{2,1,0:T(8,128)(2,1)}), bf16[8,512,256]{2,1,0:T(8,128)(2,1)S(1)}, u32[]{:S(2)}, u32[]{:S(2)}) %all-to-all-start.2) | async-done | bytes 2097184 | tf_op jit(solution)/shard_map/all_to_all | solution.py:15
  97.9 2.8 fusion.40
  100.7 1.3 fusion.7
  102.0 4.5 %all-to-all-start.5 = ((bf16[32,2,16,256]{3,2,1,0:T(8,128)(2,1)}), bf16[32,2,16,256]{3,2,1,0:T(8,128)(2,1)S(1)}, u32[]{:S(2)}, u32[]{:S(2)}) async-start(bf16[32,2,16,256]{3,2,1,0:T(8,128)(2,1)} %bitcast.15), calls=%async_computation.5 | async-start | bytes 1048576 | tf_op jit(solution)/shard_map/all_to_all | solution.py:107
  106.6 17.6 %all-to-all-done.5 = bf16[32,2,16,256]{3,2,1,0:T(8,128)(2,1)S(1)} async-done(((bf16[32,2,16,256]{3,2,1,0:T(8,128)(2,1)}), bf16[32,2,16,256]{3,2,1,0:T(8,128)(2,1)S(1)}, u32[]{:S(2)}, u32[]{:S(2)}) %all-to-all-start.5) | async-done | bytes 524320 | tf_op jit(solution)/shard_map/all_to_all | solution.py:107
  124.2 1.5 stack.9
  125.7 3.6 %all-to-all-start.4 = ((bf16[8,512,256]{1,2,0:T(8,128)(2,1)}), bf16[8,512,256]{1,2,0:T(8,128)(2,1)S(1)}, u32[]{:S(2)}, u32[]{:S(2)}) async-start(bf16[8,512,256]{1,2,0:T(8,128)(2,1)} %stack.9), calls=%async_computation.4 | async-start | bytes 4194304 | tf_op jit(solution)/shard_map/all_to_all | solution.py:15
  129.3 27.0 %all-to-all-done.4 = bf16[8,512,256]{1,2,0:T(8,128)(2,1)S(1)} async-done(((bf16[8,512,256]{1,2,0:T(8,128)(2,1)}), bf16[8,512,256]{1,2,0:T(8,128)(2,1)S(1)}, u32[]{:S(2)}, u32[]{:S(2)}) %all-to-all-start.4) | async-done | bytes 2097184 | tf_op jit(solution)/shard_map/all_to_all | solution.py:15
  156.4 2.3 stack.10
  158.7 4.7 %all-to-all-start.6 = ((bf16[8,1024,256]{2,1,0:T(8,128)(2,1)}), bf16[8,1024,256]{2,1,0:T(8,128)(2,1)}, u32[]{:S(2)}, u32[]{:S(2)}) async-start(bf16[8,1024,256]{2,1,0:T(8,128)(2,1)} %stack.10), calls=%async_computation.6 | async-start | bytes 8388608 | tf_op jit(solution)/shard_map/all_to_all | solution.py:15
  163.4 2.0 copy.72
  165.4 0.5 multiply_reduce_fusion.1
  165.9 0.5 copy-done.13
  166.4 0.7 convolution_multiply_fusion.3
  167.2 0.8 fusion.22
  168.0 45.0 %all-to-all-done.6 = bf16[8,1024,256]{2,1,0:T(8,128)(2,1)} async-done(((bf16[8,1024,256]{2,1,0:T(8,128)(2,1)}), bf16[8,1024,256]{2,1,0:T(8,128)(2,1)}, u32[]{:S(2)}, u32[]{:S(2)}) %all-to-all-start.6) | async-done | bytes 4194336 | tf_op jit(solution)/shard_map/all_to_all | solution.py:15
  213.0 3.7 %all-to-all-start.9 = ((bf16[2,128,2048]{1,0,2:T(2,128)(2,1)}), bf16[2,128,2048]{1,0,2:T(2,128)(2,1)S(1)}, u32[]{:S(2)}, u32[]{:S(2)}) async-start(bf16[2,128,2048]{1,0,2:T(2,128)(2,1)} %copy.72), calls=%async_computation.9 | async-start | bytes 2097152 | tf_op jit(solution)/shard_map/all_to_all | solution.py:75
  216.8 3.1 multiply_reduce_fusion
  219.9 6.6 %copy.68 = bf16[1024,8,256]{2,1,0:T(8,128)(2,1)} copy(bf16[1024,8,256]{2,0,1:T(8,128)(2,1)} %bitcast.18) | data formatting | bytes 8388608 | tf_op jit(solution)/shard_map/reshape | solution.py:16
  226.4 7.5 %reshape_reshape.3 = bf16[2,512,2048]{2,1,0:T(8,128)(2,1)} reshape(bf16[1024,8,256]{2,1,0:T(8,128)(2,1)} %copy.68) | data formatting | bytes 8388608 | tf_op jit(solution)/shard_map/reshape;reshape | solution.py:116
  233.9 3.6 %convolution_multiply_fusion.1 = f32[2,512,128]{2,1,0:T(8,128)S(1)} fusion(bf16[2,512,2048]{2,1,0:T(8,128)(2,1)} %reshape_reshape.3, bf16[2,2048,128]{2,1,0:T(8,128)(2,1)S(1)} %copy-done.10, f32[2,512]{1,0:T(2,128)S(1)} %rsqrt.40), kind=kOutput, calls=%fused_computation.25 | convolution fusion | flops 537001984 | bytes 5771264 | tf_op jit(solution)/shard_map/erd,edf->erf/dot_general | solution.py:117
  237.6 1.3 fusion.19
  239.0 2.1 stack.11
  241.0 4.9 %all-to-all-start.7 = ((bf16[8,1536,128]{2,1,0:T(8,128)(2,1)}), bf16[8,1536,128]{2,1,0:T(8,128)(2,1)}, u32[]{:S(2)}, u32[]{:S(2)}) async-start(bf16[8,1536,128]{2,1,0:T(8,128)(2,1)} %stack.11), calls=%async_computation.7 | async-start | bytes 6291456 | tf_op jit(solution)/shard_map/all_to_all | solution.py:15
  245.9 0.3 copy.69
  246.2 1.0 copy.70
  247.2 37.2 %all-to-all-done.7 = bf16[8,1536,128]{2,1,0:T(8,128)(2,1)} async-done(((bf16[8,1536,128]{2,1,0:T(8,128)(2,1)}), bf16[8,1536,128]{2,1,0:T(8,128)(2,1)}, u32[]{:S(2)}, u32[]{:S(2)}) %all-to-all-start.7) | async-done | bytes 3145760 | tf_op jit(solution)/shard_map/all_to_all | solution.py:15
  284.4 4.1 %all-to-all-start.8 = ((bf16[128,8,256]{2,0,1:T(8,128)(2,1)}), bf16[128,8,256]{2,0,1:T(8,128)(2,1)}, u32[]{:S(2)}, u32[]{:S(2)}) async-start(bf16[128,8,256]{2,0,1:T(8,128)(2,1)} %copy.70), calls=%async_computation.8 | async-start | bytes 1048576 | tf_op jit(solution)/shard_map/all_to_all | solution.py:29
  288.5 2.0 copy.73
  290.6 1.7 slice.11
  292.3 1.4 copy.71
  293.7 2.3 reshape.153
  296.0 2.4 convolution_convert_fusion
  298.3 0.8 copy.81
  299.2 4.9 %all-to-all-start.10 = ((bf16[32,2,16,256]{3,2,1,0:T(8,128)(2,1)}), bf16[32,2,16,256]{3,2,1,0:T(8,128)(2,1)S(1)}, u32[]{:S(2)}, u32[]{:S(2)}) async-start(bf16[32,2,16,256]{3,2,1,0:T(8,128)(2,1)} %bitcast.79), calls=%async_computation.10 | async-start | bytes 1048576 | tf_op jit(solution)/shard_map/all_to_all | solution.py:130
  304.1 1.9 fusion.15
  306.0 16.2 %all-to-all-done.10 = bf16[32,2,16,256]{3,2,1,0:T(8,128)(2,1)S(1)} async-done(((bf16[32,2,16,256]{3,2,1,0:T(8,128)(2,1)}), bf16[32,2,16,256]{3,2,1,0:T(8,128)(2,1)S(1)}, u32[]{:S(2)}, u32[]{:S(2)}) %all-to-all-start.10) | async-done | bytes 524320 | tf_op jit(solution)/shard_map/all_to_all | solution.py:130
  322.2 1.5 fusion.20
  (49 shorter events, 0.7 us)
Async XLA Ops:
  0.0 2.2 copy-start
  0.0 2.5 copy-start.5
  2.6 1.2 copy-start.15
  3.8 0.9 copy-start.7
  3.8 14.0 %copy-start.16 = (bf16[2048,256]{1,0:T(8,128)(2,1)S(1)}, bf16[2048,256]{1,0:T(8,128)(2,1)}, u32[]{:S(2)}) copy-start(bf16[2048,256]{1,0:T(8,128)(2,1)} %param.13) | copy-start | bytes 3145732
  5.6 21.2 %all-to-all-start = ((f32[32,8,128]{2,1,0:T(8,128)}), f32[32,8,128]{2,1,0:T(8,128)S(1)}, u32[]{:S(2)}, u32[]{:S(2)}) async-start(f32[32,8,128]{2,1,0:T(8,128)} %bitcast.3), calls=%async_computation | async-start | bytes 262144 | tf_op jit(solution)/shard_map/all_to_all | solution.py:40
  22.1 13.4 %copy-start.3 = (pred[512,512]{1,0:T(8,128)(4,1)S(1)}, pred[512,512]{1,0:T(8,128)(4,1)}, u32[]{:S(2)}) copy-start(pred[512,512]{1,0:T(8,128)(4,1)} %iota_compare_fusion.9) | copy-start | bytes 786436
  28.8 16.5 %all-to-all-start.1 = ((f32[32,8,128]{2,1,0:T(8,128)}), f32[32,8,128]{2,1,0:T(8,128)S(1)}, u32[]{:S(2)}, u32[]{:S(2)}) async-start(f32[32,8,128]{2,1,0:T(8,128)} %select_reduce_fusion), calls=%async_computation.1 | async-start | bytes 262144 | tf_op jit(solution)/shard_map/all_to_all | solution.py:43
  35.5 14.2 %copy-start.4 = (bf16[512,256]{0,1:T(8,128)(2,1)S(1)}, bf16[512,256]{0,1:T(8,128)(2,1)}, u32[]{:S(2)}) copy-start(bf16[512,256]{0,1:T(8,128)(2,1)} %convolution_convert_fusion.2) | copy-start | bytes 786436
  45.3 20.3 %all-to-all-start.3 = ((bf16[256,8,256]{2,0,1:T(8,128)(2,1)}), bf16[256,8,256]{2,0,1:T(8,128)(2,1)}, u32[]{:S(2)}, u32[]{:S(2)}) async-start(bf16[256,8,256]{2,0,1:T(8,128)(2,1)} %copy.65), calls=%async_computation.3 | async-start | bytes 2097152 | tf_op jit(solution)/shard_map/all_to_all | solution.py:29
  49.7 1.0 copy-start.6
  67.1 3.8 %copy-start.14 = (s32[512,1]{0,1:T(1,128)S(1)}, s32[512,1]{0,1:T(1,128)}, u32[]{:S(2)}) copy-start(s32[512,1]{0,1:T(1,128)} %param.23) | copy-start | bytes 6148
  67.1 30.8 %all-to-all-start.2 = ((bf16[8,512,256]{2,1,0:T(8,128)(2,1)}), bf16[8,512,256]{2,1,0:T(8,128)(2,1)S(1)}, u32[]{:S(2)}, u32[]{:S(2)}) async-start(bf16[8,512,256]{2,1,0:T(8,128)(2,1)} %stack.8), calls=%async_computation.2 | async-start | bytes 4194304 | tf_op jit(solution)/shard_map/all_to_all | solution.py:15
  102.0 22.2 %all-to-all-start.5 = ((bf16[32,2,16,256]{3,2,1,0:T(8,128)(2,1)}), bf16[32,2,16,256]{3,2,1,0:T(8,128)(2,1)S(1)}, u32[]{:S(2)}, u32[]{:S(2)}) async-start(bf16[32,2,16,256]{3,2,1,0:T(8,128)(2,1)} %bitcast.15), calls=%async_computation.5 | async-start | bytes 1048576 | tf_op jit(solution)/shard_map/all_to_all | solution.py:107
  125.7 30.7 %all-to-all-start.4 = ((bf16[8,512,256]{1,2,0:T(8,128)(2,1)}), bf16[8,512,256]{1,2,0:T(8,128)(2,1)S(1)}, u32[]{:S(2)}, u32[]{:S(2)}) async-start(bf16[8,512,256]{1,2,0:T(8,128)(2,1)} %stack.9), calls=%async_computation.4 | async-start | bytes 4194304 | tf_op jit(solution)/shard_map/all_to_all | solution.py:15
  158.7 4.7 %copy-start.8 = (bf16[2,128,2048]{2,1,0:T(8,128)(2,1)S(1)}, bf16[2,128,2048]{2,1,0:T(8,128)(2,1)}, u32[]{:S(2)}) copy-start(bf16[2,128,2048]{2,1,0:T(8,128)(2,1)} %param.22) | copy-start | bytes 3145732
  158.7 54.3 %all-to-all-start.6 = ((bf16[8,1024,256]{2,1,0:T(8,128)(2,1)}), bf16[8,1024,256]{2,1,0:T(8,128)(2,1)}, u32[]{:S(2)}, u32[]{:S(2)}) async-start(bf16[8,1024,256]{2,1,0:T(8,128)(2,1)} %stack.10), calls=%async_computation.6 | async-start | bytes 8388608 | tf_op jit(solution)/shard_map/all_to_all | solution.py:15
  165.4 1.0 copy-start.13
  165.4 1.8 copy-start.18
  213.0 25.9 %all-to-all-start.9 = ((bf16[2,128,2048]{1,0,2:T(2,128)(2,1)}), bf16[2,128,2048]{1,0,2:T(2,128)(2,1)S(1)}, u32[]{:S(2)}, u32[]{:S(2)}) async-start(bf16[2,128,2048]{1,0,2:T(2,128)(2,1)} %copy.72), calls=%async_computation.9 | async-start | bytes 2097152 | tf_op jit(solution)/shard_map/all_to_all | solution.py:75
  226.4 7.5 %copy-start.10 = (bf16[2,2048,128]{2,1,0:T(8,128)(2,1)S(1)}, bf16[2,2048,128]{2,1,0:T(8,128)(2,1)}, u32[]{:S(2)}) copy-start(bf16[2,2048,128]{2,1,0:T(8,128)(2,1)} %param.20) | copy-start | bytes 3145732
  233.9 3.6 %copy-start.2 = (bf16[2,512,2048]{2,1,0:T(8,128)(2,1)S(1)}, bf16[2,512,2048]{2,1,0:T(8,128)(2,1)}, u32[]{:S(2)}) copy-start(bf16[2,512,2048]{2,1,0:T(8,128)(2,1)} %reshape_reshape.3) | copy-start | bytes 12582916
  233.9 3.7 %copy-start.17 = (bf16[2,2048,128]{2,1,0:T(8,128)(2,1)S(1)}, bf16[2,2048,128]{2,1,0:T(8,128)(2,1)}, u32[]{:S(2)}) copy-start(bf16[2,2048,128]{2,1,0:T(8,128)(2,1)} %param.21) | copy-start | bytes 3145732
  241.0 4.9 %copy-start.12 = (bf16[128,2048]{1,0:T(8,128)(2,1)S(1)}, bf16[128,2048]{1,0:T(8,128)(2,1)}, u32[]{:S(2)}) copy-start(bf16[128,2048]{1,0:T(8,128)(2,1)} %param.19) | copy-start | bytes 1572868
  241.0 43.4 %all-to-all-start.7 = ((bf16[8,1536,128]{2,1,0:T(8,128)(2,1)}), bf16[8,1536,128]{2,1,0:T(8,128)(2,1)}, u32[]{:S(2)}, u32[]{:S(2)}) async-start(bf16[8,1536,128]{2,1,0:T(8,128)(2,1)} %stack.11), calls=%async_computation.7 | async-start | bytes 6291456 | tf_op jit(solution)/shard_map/all_to_all | solution.py:15
  284.4 14.8 %all-to-all-start.8 = ((bf16[128,8,256]{2,0,1:T(8,128)(2,1)}), bf16[128,8,256]{2,0,1:T(8,128)(2,1)}, u32[]{:S(2)}, u32[]{:S(2)}) async-start(bf16[128,8,256]{2,0,1:T(8,128)(2,1)} %copy.70), calls=%async_computation.8 | async-start | bytes 1048576 | tf_op jit(solution)/shard_map/all_to_all | solution.py:29
  293.7 2.3 copy-start.9
  296.0 8.1 %copy-start.11 = (f32[512,256]{1,0:T(8,128)S(1)}, f32[512,256]{1,0:T(8,128)}, u32[]{:S(2)}) copy-start(f32[512,256]{1,0:T(8,128)} %get-tuple-element.8) | copy-start | bytes 1572868
  299.2 23.1 %all-to-all-start.10 = ((bf16[32,2,16,256]{3,2,1,0:T(8,128)(2,1)}), bf16[32,2,16,256]{3,2,1,0:T(8,128)(2,1)S(1)}, u32[]{:S(2)}, u32[]{:S(2)}) async-start(bf16[32,2,16,256]{3,2,1,0:T(8,128)(2,1)} %bitcast.79), calls=%async_computation.10 | async-start | bytes 1048576 | tf_op jit(solution)/shard_map/all_to_all | solution.py:130
  304.1 19.7 %copy-start.1 = (bf16[2048,256]{1,0:T(8,128)(2,1)S(1)}, bf16[2048,256]{1,0:T(8,128)(2,1)}, u32[]{:S(2)}) copy-start(bf16[2048,256]{1,0:T(8,128)(2,1)} %param.14) | copy-start | bytes 3145732
